TPU v7x, 128 devices: a whole 4x4x4 slice. The times are simulated.
128 devices in a mesh: seq: 32 (over z, y, core), tp: 4 (over x).
Axes of the slice: x: 4, y: 4, z: 4, core: 2. Of those that a mesh axis runs over, the one named last changes fastest.
Arguments:
- states: bfloat16 [256, 3072], P(None, 'seq'), may hold values from -20 to 20
- norm_gain: bfloat16 [3072], P('seq'), may hold values from 0.25 to 1.75
- w_qkv: bfloat16 [3, 3072, 3072], P(None, 'seq', 'tp'), may hold values from -0.109375 to 0.109375
- w_out: bfloat16 [3072, 3072], P('tp', 'seq'), may hold values from -0.109375 to 0.109375
- cache: bfloat16 [768, 2, 64, 3072], P('seq', None, None, 'tp'), may hold values from -400 to 400
- context_len: int32 [256], replicated, may hold values from 1 to 4096, as said below
- block_owner: int32 [768], P('seq'), may hold values from 0 to 256, as said below
- block_index: int32 [768], P('seq'), may hold values from 0 to 63, as said below
Outputs:
- hidden: bfloat16 [256, 3072], P('tp', 'seq')
- updated: bfloat16 [768, 2, 64, 3072], P('seq', None, None, 'tp')
Inputs may be any that keep to these rules, and one draw needn't show every extreme that they name: `context_len`: A request of length n owns exactly ceil(n / 64) pool blocks, with block_index 0, 1, ... once each; at least one pool block is unused. `context_len`: exactly 4 requests own 64/2 blocks or more; every other request owns at most 2 blocks, all on one index of seq. `block_owner`: the value 256 marks an unused block. `block_index`: 0 for an unused block.
All inputs are finite; a program needn't handle non-finite values.
Results may differ from a plain program's by a relative error of at most 0.0068.
Values may be sent and summed in bfloat16 or wider, within the bound.
A program may use at most 128 MiB of HBM per device.

v0:
```python
import jax
import jax.numpy as jnp
from jax import lax
from jax.sharding import PartitionSpec as P

HEAD_DIM = 96
EPSILON = 1e-05
NEG_FLOOR = -1e30


def combined_all(part, axis, combine):
    gathered = jax.tree.map(lambda a: lax.all_gather(a, axis), part)

    def take(source):
        return jax.tree.map(lambda a: lax.dynamic_index_in_dim(a, source, 0, False), gathered)

    return lax.fori_loop(
        1, lax.axis_size(axis), lambda source, state: combine(state, take(source)), take(0)
    )


def rotate(values, positions):
    half_dim = HEAD_DIM // 2
    frequency = 10000.0 ** (-jnp.arange(half_dim, dtype=jnp.float32) * 2.0 / HEAD_DIM)
    angles = positions.astype(jnp.float32)[:, None] * frequency[None, :]
    cosine = jnp.cos(angles)[:, None, :]
    sine_part = jnp.sin(angles)[:, None, :]
    front_half = values[..., :half_dim]
    back_half = values[..., half_dim:]
    return jnp.concatenate(
        [front_half * cosine - back_half * sine_part, back_half * cosine + front_half * sine_part],
        axis=-1,
    )


def finish(projected, positions):
    row_count = projected.shape[0]
    columns = projected.shape[2]
    head_count = columns // HEAD_DIM
    query = rotate(
        projected[:, 0].reshape(row_count, head_count, HEAD_DIM), positions
    ) * HEAD_DIM ** (-0.5)
    keys_new = rotate(projected[:, 1].reshape(row_count, head_count, HEAD_DIM), positions)
    return (
        query.astype(jnp.bfloat16).reshape(row_count, columns),
        keys_new.astype(jnp.bfloat16).reshape(row_count, columns),
        projected[:, 2].astype(jnp.bfloat16),
    )


def join(earlier, later):
    highest = jnp.maximum(earlier[0], later[0])
    left_scale = jnp.exp(earlier[0] - highest)
    right_scale = jnp.exp(later[0] - highest)
    return (
        highest,
        earlier[1] * left_scale + later[1] * right_scale,
        earlier[2] * jnp.repeat(left_scale, HEAD_DIM, axis=1)
        + later[2] * jnp.repeat(right_scale, HEAD_DIM, axis=1),
    )


def shards(states, norm_gain, w_qkv, w_out, cache, context_len, block_owner, block_index):
    requests = states.shape[0]
    seq_count = lax.axis_size("seq")
    wide_states = states.astype(jnp.float32)
    sum_squares = lax.psum(jnp.sum(wide_states * wide_states, axis=1), "seq")
    inverse = lax.rsqrt(sum_squares / (states.shape[1] * seq_count) + EPSILON)
    normed = (wide_states * inverse[:, None] * norm_gain.astype(jnp.float32)[None, :]).astype(
        jnp.bfloat16
    )
    positions = context_len - 1
    local_term = jnp.einsum("rd,cdh->rch", normed, w_qkv, preferred_element_type=jnp.float32)
    projected = lax.psum(local_term, "seq")
    query, keys_new, values_new = finish(projected, positions)
    blocks, _, tokens, columns = cache.shape
    head_count = columns // HEAD_DIM
    block_live = block_owner < requests
    owner_row = jnp.minimum(block_owner, requests - 1)
    last_position = positions[owner_row]
    block_hit = block_live & (block_index == last_position // tokens)
    slot_hit = block_hit[:, None] & (
        jnp.arange(tokens, dtype=jnp.int32)[None, :] == (last_position % tokens)[:, None]
    )
    fresh_rows = jnp.stack([keys_new[owner_row], values_new[owner_row]], axis=1)
    updated = jnp.where(slot_hit[:, None, :, None], fresh_rows[:, :, None, :], cache)
    query_rows = query[owner_row].reshape(blocks, head_count, HEAD_DIM)
    key_cache = updated[:, 0].reshape(blocks, tokens, head_count, HEAD_DIM)
    value_cache = updated[:, 1].reshape(blocks, tokens, head_count, HEAD_DIM)
    scores = jnp.einsum("bhd,bthd->bht", query_rows, key_cache, preferred_element_type=jnp.float32)
    token_position = block_index[:, None] * tokens + jnp.arange(tokens, dtype=jnp.int32)[None, :]
    visible = block_live[:, None] & (token_position < context_len[owner_row][:, None])
    masked = jnp.where(visible[:, None, :], scores, NEG_FLOOR)
    block_max = jnp.max(masked, axis=-1)
    weights = jnp.where(visible[:, None, :], jnp.exp(masked - block_max[..., None]), 0.0).astype(
        jnp.bfloat16
    )
    block_sum = jnp.sum(weights.astype(jnp.float32), axis=-1)
    block_out = jnp.einsum(
        "bht,bthd->bhd", weights, value_cache, preferred_element_type=jnp.float32
    ).reshape(blocks, columns)
    segment = jnp.where(block_live, block_owner, requests)
    member = segment[None, :] == jnp.arange(requests, dtype=jnp.int32)[:, None]
    local_max = jnp.max(jnp.where(member[:, :, None], block_max[None, :, :], NEG_FLOOR), axis=1)
    factor = jnp.exp(block_max - local_max[owner_row])
    member_matrix = member.astype(jnp.float32)
    totals = jnp.dot(member_matrix, block_sum * factor, precision=lax.Precision.HIGHEST)
    outputs = jnp.dot(
        member_matrix,
        block_out * jnp.repeat(factor, HEAD_DIM, axis=1),
        precision=lax.Precision.HIGHEST,
    )
    merged = combined_all((local_max, totals, outputs), "seq", join)
    attended = (merged[2] / jnp.repeat(merged[1], HEAD_DIM, axis=1)).astype(jnp.bfloat16)
    terms = jnp.dot(attended, w_out, preferred_element_type=jnp.float32)
    summed = lax.psum_scatter(terms, "tp", scatter_dimension=0, tiled=True)
    row_count = summed.shape[0]
    residual_rows = lax.dynamic_slice_in_dim(
        wide_states, lax.axis_index("tp") * row_count, row_count, 0
    )
    hidden = (summed + residual_rows).astype(jnp.bfloat16)
    return (hidden, updated)


def solution(mesh):
    return jax.shard_map(
        shards,
        mesh=mesh,
        in_specs=(
            P(None, "seq"),
            P("seq"),
            P(None, "seq", "tp"),
            P("tp", "seq"),
            P("seq", None, None, "tp"),
            P(),
            P("seq"),
            P("seq"),
        ),
        out_specs=(P("tp", "seq"), P("seq", None, None, "tp")),
        check_vma=False,
    )
```

profile of v0, /device:TPU:0, one launch (start us, length us, event | category | flops | bytes accessed | tf_op | source)
XLA Modules:
  0.0 399.5 jit_solution(8305740966183515385)
XLA Ops:
  8.1 68.7 %psum.14 = f32[256]{0:T(256)S(1)} all-reduce(f32[256]{0:T(256)S(1)} %multiply_reduce_fusion), channel_id=1, replica_groups=mesh['seq'=32,'tp'=4] {'seq'}, use_global_device_ids=true, to_apply=%region_1.0 | all-reduce | flops 256 | bytes 2048 | tf_op jit(solution)/shard_map/psum | solution.py:67
  77.5 2.8 fusion.12
  82.3 102.0 %all-reduce.2.cloned.1.call-done = f32[256,3,768]{2,0,1:T(8,128)} async-done(((f32[256,3,768]{2,0,1:T(8,128)}), f32[256,3,768]{2,0,1:T(8,128)}) %all-reduce.2.cloned.1.call-update) | async-done | bytes 2359312 | tf_op jit(solution)/shard_map/psum | solution.py:74
  184.3 1.5 fusion.28
  190.1 2.7 broadcast_select_fusion
  192.8 2.2 fusion.27
  195.7 6.4 %reshape_squeeze.14 = bf16[24,64,8,96]{3,2,1,0:T(8,128)(2,1)} reshape(bf16[24,1,64,768]{3,2,1,0:T(8,128)(2,1)} %get-tuple-element.239) | data formatting | bytes 4718592 | tf_op jit(solution)/shard_map/reshape;squeeze | solution.py:88
  204.3 1.7 gather_fusion.1
  206.1 3.6 fusion.5
  210.0 4.3 %reshape_squeeze.15 = bf16[24,64,8,96]{3,2,1,0:T(8,128)(2,1)} reshape(bf16[24,1,64,768]{3,2,1,0:T(8,128)(2,1)S(1)} %get-tuple-element.238) | data formatting | bytes 4718592 | tf_op jit(solution)/shard_map/reshape;squeeze | solution.py:89
  215.1 2.8 fusion.3
  218.1 1.5 fusion.17
  219.9 25.3 %all-gather.1 = f32[8192,8]{0,1:T(8,128)S(1)} all-gather(f32[256,8]{0,1:T(8,128)S(1)} %fusion.18), channel_id=3, replica_groups=mesh['seq'=32,'tp'=4] {'seq'}, dimensions={0}, use_global_device_ids=true | all-gather | bytes 270336 | tf_op jit(solution)/shard_map/all_gather | solution.py:12
  245.2 22.3 %all-gather = f32[8192,8]{0,1:T(8,128)S(1)} all-gather(f32[256,8]{0,1:T(8,128)S(1)} %select_reduce_fusion), channel_id=2, replica_groups=mesh['seq'=32,'tp'=4] {'seq'}, dimensions={0}, use_global_device_ids=true | all-gather | bytes 270336 | tf_op jit(solution)/shard_map/all_gather | solution.py:12
  267.5 44.9 %all-gather.5.cloned.1.call-done = f32[8192,768]{1,0:T(8,128)} async-done(((f32[256,768]{1,0:T(8,128)}), f32[8192,768]{1,0:T(8,128)}) %all-gather.5.cloned.1.call-update) | async-done | bytes 25165840 | tf_op jit(solution)/shard_map/all_gather | solution.py:12
  313.9 56.6 %while.19 = (s32[]{:T(128)}, f32[256,8]{0,1:T(8,128)S(1)}, f32[256,8]{0,1:T(8,128)S(1)}, f32[256,768]{0,1:T(8,128)S(1)}, f32[32,256,8]{1,2,0:T(8,128)S(1)}, /*in...) while((s32[]{:T(128)}, f32[256,8]{0,1:T(8,128)S(1)}, ...), condition=%wide.region_7.8_spmd, body=%wide.region_6.7_spmd.sunk | while | flops 602117 | bytes 5587095 | solution.py:17
  314.0 1.2 constant_dynamic-slice_fusion.2
  317.7 1.2 constant_dynamic-slice_fusion.2
  321.3 1.2 constant_dynamic-slice_fusion.2
  325.0 1.2 constant_dynamic-slice_fusion.2
  328.6 1.2 constant_dynamic-slice_fusion.2
  332.2 1.2 constant_dynamic-slice_fusion.2
  334.1 1.2 constant_dynamic-slice_fusion.2
  371.6 19.7 %reduce-scatter.4.cloned.1.call-done = f32[64,96]{1,0:T(8,128)} async-done(((f32[256,96]{1,0:T(8,128)}), f32[64,96]{1,0:T(8,128)}) %reduce-scatter.4.cloned.1.call-update) | async-done | bytes 24592
  (184 shorter events, 63.4 us)
Async XLA Ops:
  7.2 70.3 %copy-start = (bf16[3,96,768]{2,1,0:T(8,128)(2,1)S(1)}, bf16[3,96,768]{2,1,0:T(8,128)(2,1)}, u32[]{:S(2)}) copy-start(bf16[3,96,768]{2,1,0:T(8,128)(2,1)} %param.12) | copy-start | bytes 1327108
  7.2 73.1 %copy-start.1 = (s32[256]{0:T(256)S(1)}, s32[256]{0:T(256)}, u32[]{:S(2)}) copy-start(s32[256]{0:T(256)} %param.15) | copy-start | bytes 3076
  7.2 73.1 %copy-start.5 = (s32[24]{0:T(128)S(1)}, s32[24]{0:T(128)}, u32[]{:S(2)}) copy-start(s32[24]{0:T(128)} %param.16) | copy-start | bytes 292
  7.2 177.1 %all-reduce.2.cloned.1.call-start = ((), (), s32[]{:S(2)}) async-start(), calls=%async_computation.1 | async-start | bytes 4718592 | tf_op jit(solution)/shard_map/psum | solution.py:74
  8.1 73.7 %copy-start.6 = (s32[24]{0:T(128)S(1)}, s32[24]{0:T(128)}, u32[]{:S(2)}) copy-start(s32[24]{0:T(128)} %param.17) | copy-start | bytes 292
  80.3 232.2 %all-gather.5.cloned.1.call-start = ((), (), s32[]{:S(2)}) async-start(), calls=%async_computation.2 | async-start | bytes 25952256 | tf_op jit(solution)/shard_map/all_gather | solution.py:12
  192.8 2.9 copy-start.2
  219.7 171.6 %reduce-scatter.4.cloned.1.call-start = ((), (), s32[]{:S(2)}) async-start(), calls=%async_computation.3 | async-start | bytes 163840
  313.9 56.7 %copy-start.4 = (bf16[768,96]{0,1:T(8,128)(2,1)S(1)}, bf16[768,96]{0,1:T(8,128)(2,1)}, u32[]{:S(2)}) copy-start(bf16[768,96]{0,1:T(8,128)(2,1)} %param.13) | copy-start | bytes 442372
  313.9 57.7 %copy-start.3 = (bf16[256,96]{0,1:T(8,128)(2,1)S(1)}, bf16[256,96]{0,1:T(8,128)(2,1)}, u32[]{:S(2)}) copy-start(bf16[256,96]{0,1:T(8,128)(2,1)} %param.10) | copy-start | bytes 147460
Sparse Core Ops, SparseCore 0:
  80.4 103.8 all-reduce.1
  219.8 92.5 all-gather.4
  371.7 19.5 reduce-scatter.3
where the time goes:
time: 402 us; the launch traced here: 399 us
  waiting for transfers between devices  167 us (42%)
  blocking collectives  116 us (29%)
  local copies, waits for them, and re-layouts  71.3 us (18%)
  other arithmetic  18 us (4%)
  between operations  14.1 us (4%)
  matrix products  11.8 us (3%)
    psum x1, waiting for transfers between devices, shards(): projected = lax.psum(local_term, 'seq')  102 us
    psum x1, blocking collectives, shards(): sum_squares = lax.psum(jnp.sum(wide_states * wide_states, axis=1), 'seq')  68.7 us
    all_gather x2, blocking collectives, combined_all(): gathered = jax.tree.map(lambda a: lax.all_gather(a, axis), part)  47.6 us
    dynamic_slice x65, local copies, waits for them, and re-layouts, take(): lax.dynamic_index_in_dim(a, source, 0, False)  46.3 us
    all_gather x1, waiting for transfers between devices, combined_all(): gathered = jax.tree.map(lambda a: lax.all_gather(a, axis), part)  44.9 us
    unnamed x4, waiting for transfers between devices  19.8 us
    add x31, other arithmetic, join(): earlier[2] * jnp.repeat(left_scale, HEAD_DIM, axis=1)  9.66 us
  transfers between devices with their start and end apart: 3, of which 3 were waited for; matrix products, arithmetic and copies ran while one was open for 1% of the time, Pallas kernels for 0%

commit v1 on v0

--- a/solution.py
+++ b/solution.py
@@ -64,7 +64,7 @@
     requests = states.shape[0]
     seq_count = lax.axis_size("seq")
     wide_states = states.astype(jnp.float32)
-    sum_squares = lax.psum(jnp.sum(wide_states * wide_states, axis=1), "seq")
+    sum_squares = jnp.sum(lax.all_gather(jnp.sum(wide_states * wide_states, axis=1), "seq"), axis=0)
     inverse = lax.rsqrt(sum_squares / (states.shape[1] * seq_count) + EPSILON)
     normed = (wide_states * inverse[:, None] * norm_gain.astype(jnp.float32)[None, :]).astype(
         jnp.bfloat16

time: 402 us -> 361 us (0.90)
  blocking collectives: 116 us -> 73.3 us
    psum x1 -> x0, blocking collectives: 68.7 us -> none  [shards(): sum_squares = lax.psum(jnp.sum(wide_states * wide_states, axis=1), 'seq')]
    all_gather x0 -> x1, blocking collectives: none -> 25.7 us  [shards(): lax.all_gather(jnp.sum(wide_states * wide_states, axis=1), 'seq')]
where the time goes in v1:
time: 361 us; the launch traced here: 359 us
  waiting for transfers between devices  170 us (47%)
  blocking collectives  73.3 us (20%)
  local copies, waits for them, and re-layouts  71.3 us (20%)
  other arithmetic  18 us (5%)
  between operations  14.1 us (4%)
  matrix products  11.8 us (3%)
    psum x1, waiting for transfers between devices, shards(): projected = lax.psum(local_term, 'seq')  105 us
    all_gather x2, blocking collectives, combined_all(): gathered = jax.tree.map(lambda a: lax.all_gather(a, axis), part)  47.6 us
    dynamic_slice x65, local copies, waits for them, and re-layouts, take(): lax.dynamic_index_in_dim(a, source, 0, False)  46.3 us
    all_gather x1, waiting for transfers between devices, combined_all(): gathered = jax.tree.map(lambda a: lax.all_gather(a, axis), part)  44.9 us
    all_gather x1, blocking collectives, shards(): lax.all_gather(jnp.sum(wide_states * wide_states, axis=1), 'seq')  25.7 us
    unnamed x4, waiting for transfers between devices  19.7 us
    add x31, other arithmetic, join(): earlier[2] * jnp.repeat(left_scale, HEAD_DIM, axis=1)  9.66 us
  transfers between devices with their start and end apart: 3, of which 3 were waited for; matrix products, arithmetic and copies ran while one was open for 1% of the time, Pallas kernels for 0%

profile of v1, /device:TPU:0, one launch (start us, length us, event | category | flops | bytes accessed | tf_op | source)
XLA Modules:
  0.0 359.5 jit_solution(6453313781373265771)
XLA Ops:
  8.1 25.7 %all-gather.4 = f32[32,1,256]{2,1,0:T(1,128)S(1)} all-gather(f32[1,1,256]{2,1,0:T(1,128)S(1)} %bitcast.76), channel_id=2, replica_groups=mesh['seq'=32,'tp'=4] {'seq'}, dimensions={0}, use_global_device_ids=true | all-gather | bytes 33792 | tf_op jit(solution)/shard_map/all_gather | solution.py:67
  34.6 2.8 fusion.12
  39.4 104.9 %all-reduce.2.cloned.1.call-done = f32[256,3,768]{2,0,1:T(8,128)} async-done(((f32[256,3,768]{2,0,1:T(8,128)}), f32[256,3,768]{2,0,1:T(8,128)}) %all-reduce.2.cloned.1.call-update) | async-done | bytes 2359312 | tf_op jit(solution)/shard_map/psum | solution.py:74
  144.3 1.5 fusion.28
  150.1 2.7 broadcast_select_fusion
  152.8 2.2 fusion.27
  155.7 6.4 %reshape_squeeze.14 = bf16[24,64,8,96]{3,2,1,0:T(8,128)(2,1)} reshape(bf16[24,1,64,768]{3,2,1,0:T(8,128)(2,1)} %get-tuple-element.246) | data formatting | bytes 4718592 | tf_op jit(solution)/shard_map/reshape;squeeze | solution.py:88
  164.3 1.7 gather_fusion.1
  166.1 3.6 %fusion.5 = f32[24,8,1,64]{3,2,1,0:T(1,128)S(1)} fusion(bf16[24,8,96,1]{2,3,1,0:T(2,128)(2,1)S(1)} %reshape.285, bf16[24,64,8,96]{3,2,1,0:T(8,128)(2,1)} %reshape_squeeze.14), kind=kOutput, calls=%fused_computation.19 | convolution fusion | flops 2359296 | bytes 2445312 | tf_op jit(solution)/shard_map/bhd,bthd->bht/dot_general | solution.py:90
  170.0 4.3 %reshape_squeeze.15 = bf16[24,64,8,96]{3,2,1,0:T(8,128)(2,1)} reshape(bf16[24,1,64,768]{3,2,1,0:T(8,128)(2,1)S(1)} %get-tuple-element.245) | data formatting | bytes 4718592 | tf_op jit(solution)/shard_map/reshape;squeeze | solution.py:89
  175.1 2.8 fusion.3
  178.1 1.5 fusion.17
  179.9 25.3 %all-gather.2 = f32[8192,8]{0,1:T(8,128)S(1)} all-gather(f32[256,8]{0,1:T(8,128)S(1)} %fusion.18), channel_id=4, replica_groups=mesh['seq'=32,'tp'=4] {'seq'}, dimensions={0}, use_global_device_ids=true | all-gather | bytes 270336 | tf_op jit(solution)/shard_map/all_gather | solution.py:12
  205.2 22.3 %all-gather.1 = f32[8192,8]{0,1:T(8,128)S(1)} all-gather(f32[256,8]{0,1:T(8,128)S(1)} %select_reduce_fusion), channel_id=3, replica_groups=mesh['seq'=32,'tp'=4] {'seq'}, dimensions={0}, use_global_device_ids=true | all-gather | bytes 270336 | tf_op jit(solution)/shard_map/all_gather | solution.py:12
  227.5 44.9 %all-gather.7.cloned.1.call-done = f32[8192,768]{1,0:T(8,128)} async-done(((f32[256,768]{1,0:T(8,128)}), f32[8192,768]{1,0:T(8,128)}) %all-gather.7.cloned.1.call-update) | async-done | bytes 25165840 | tf_op jit(solution)/shard_map/all_gather | solution.py:12
  273.9 56.6 %while.19 = (s32[]{:T(128)}, f32[256,8]{0,1:T(8,128)S(1)}, f32[256,8]{0,1:T(8,128)S(1)}, f32[256,768]{0,1:T(8,128)S(1)}, f32[32,256,8]{1,2,0:T(8,128)S(1)}, /*in...) while((s32[]{:T(128)}, f32[256,8]{0,1:T(8,128)S(1)}, ...), condition=%wide.region_7.8_spmd, body=%wide.region_6.7_spmd.sunk | while | flops 602117 | bytes 5587095 | solution.py:17
  274.0 1.2 constant_dynamic-slice_fusion.2
  275.8 1.2 constant_dynamic-slice_fusion.2
  277.7 1.2 constant_dynamic-slice_fusion.2
  281.3 1.2 constant_dynamic-slice_fusion.2
  284.9 1.2 constant_dynamic-slice_fusion.2
  288.6 1.2 constant_dynamic-slice_fusion.2
  292.2 1.2 constant_dynamic-slice_fusion.2
  331.6 19.7 %reduce-scatter.4.cloned.1.call-done = f32[64,96]{1,0:T(8,128)} async-done(((f32[256,96]{1,0:T(8,128)}), f32[64,96]{1,0:T(8,128)}) %reduce-scatter.4.cloned.1.call-update) | async-done | bytes 24592
  (185 shorter events, 63.5 us)
Async XLA Ops:
  7.2 27.4 %copy-start = (bf16[3,96,768]{2,1,0:T(8,128)(2,1)S(1)}, bf16[3,96,768]{2,1,0:T(8,128)(2,1)}, u32[]{:S(2)}) copy-start(bf16[3,96,768]{2,1,0:T(8,128)(2,1)} %param.12) | copy-start | bytes 1327108
  7.2 30.2 %copy-start.1 = (s32[256]{0:T(256)S(1)}, s32[256]{0:T(256)}, u32[]{:S(2)}) copy-start(s32[256]{0:T(256)} %param.15) | copy-start | bytes 3076
  7.2 30.3 %copy-start.5 = (s32[24]{0:T(128)S(1)}, s32[24]{0:T(128)}, u32[]{:S(2)}) copy-start(s32[24]{0:T(128)} %param.16) | copy-start | bytes 292
  7.2 137.1 %all-reduce.2.cloned.1.call-start = ((), (), s32[]{:S(2)}) async-start(), calls=%async_computation.1 | async-start | bytes 4718592 | tf_op jit(solution)/shard_map/psum | solution.py:74
  33.9 5.0 %copy-start.6 = (s32[24]{0:T(128)S(1)}, s32[24]{0:T(128)}, u32[]{:S(2)}) copy-start(s32[24]{0:T(128)} %param.17) | copy-start | bytes 292
  37.4 235.1 %all-gather.7.cloned.1.call-start = ((), (), s32[]{:S(2)}) async-start(), calls=%async_computation.2 | async-start | bytes 25952256 | tf_op jit(solution)/shard_map/all_gather | solution.py:12
  152.8 2.9 copy-start.2
  179.7 171.6 %reduce-scatter.4.cloned.1.call-start = ((), (), s32[]{:S(2)}) async-start(), calls=%async_computation.3 | async-start | bytes 163840
  273.9 56.7 %copy-start.4 = (bf16[768,96]{0,1:T(8,128)(2,1)S(1)}, bf16[768,96]{0,1:T(8,128)(2,1)}, u32[]{:S(2)}) copy-start(bf16[768,96]{0,1:T(8,128)(2,1)} %param.13) | copy-start | bytes 442372
  273.9 57.7 %copy-start.3 = (bf16[256,96]{0,1:T(8,128)(2,1)S(1)}, bf16[256,96]{0,1:T(8,128)(2,1)}, u32[]{:S(2)}) copy-start(bf16[256,96]{0,1:T(8,128)(2,1)} %param.10) | copy-start | bytes 147460
Sparse Core Ops, SparseCore 0:
  37.5 106.7 all-reduce.1
  179.8 92.6 all-gather.6
  331.7 19.5 reduce-scatter.3
